TPU v7x, 512 devices: a whole 4x4x16 slice. The times are simulated.
512 devices in a mesh: dp: 16 (over z), row: 8 (over y, core), col: 4 (over x).
Axes of the slice: x: 4, y: 4, z: 16, core: 2. Of those that a mesh axis runs over, the one named last changes fastest.
Arguments:
- grad_blocks: bfloat16 [16, 4096, 1024], P('dp', 'row', 'col'), may hold values from -300 to 300
- ln_grads: bfloat16 [16, 4, 1024], P('dp', None, 'col'), may hold values from -240 to 240, as said below
- master: float32 [4096, 1024], P(('row', 'col')), may hold values from -6 to 6
- first_moment: float32 [4096, 1024], P(('row', 'col')), may hold values from -6 to 6
- second_moment: float32 [4096, 1024], P(('row', 'col')), may hold values from 0.3 to 3
- average: float32 [4096, 1024], P('row', 'col'), may hold values from -6 to 6
- ln_master: float32 [4, 1024], P(None, 'col'), may hold values from -6 to 6
- ln_first: float32 [4, 1024], P(None, 'col'), may hold values from -6 to 6
- ln_second: float32 [4, 1024], P(None, 'col'), may hold values from 0.3 to 3
- ln_average: float32 [4, 1024], P(None, 'col'), may hold values from -6 to 6
Outputs:
- average_new: float32 [4096, 1024], P('row', 'col')
- master_new: float32 [4096, 1024], P(('row', 'col'))
- first_new: float32 [4096, 1024], P(('row', 'col'))
- second_new: float32 [4096, 1024], P(('row', 'col'))
- ln_master_new: float32 [4, 1024], P(None, 'col')
- ln_first_new: float32 [4, 1024], P(None, 'col')
- ln_second_new: float32 [4, 1024], P(None, 'col')
- ln_average_new: float32 [4, 1024], P(None, 'col')
Inputs may be any that keep to these rules, and one draw needn't show every extreme that they name: `ln_grads`: partial gradients of each data-parallel group.
All inputs are finite; a program needn't handle non-finite values.
Results may differ from a plain program's by a relative error of at most 0.0003.
Values may be sent and summed in bfloat16 or wider, within the bound.
A program may use at most 64 MiB of HBM per device.

v0:
```python
import math
import jax
import jax.numpy as jnp
from jax import lax
from jax.sharding import PartitionSpec as P

D = 1024
FF = 4096
STEP = 20
beta_one = 0.9
beta_two = 0.95
learn_rate = 0.02
decay_rate = 0.1
epsilon = 1e-08
clip_rms = 1.0
ema_keep = 0.9


def adam_step(gradient, clip_scale, first, second, master, decay_weight):
    clipped = clip_scale * gradient
    first_new = beta_one * first + (1.0 - beta_one) * clipped
    second_new = beta_two * second + (1.0 - beta_two) * clipped * clipped
    direction = (
        first_new
        / (1.0 - beta_one**STEP)
        / (jnp.sqrt(second_new / (1.0 - beta_two**STEP)) + epsilon)
    )
    master_new = master - learn_rate * (direction + decay_weight * master)
    return (master_new, first_new, second_new)


def clip_factor(norm_total):
    return jnp.minimum(1.0, clip_rms * math.sqrt(FF * D + 4 * D) / jnp.sqrt(norm_total))


def squares(gradient, ln_gradient, row_count):
    return jnp.sum(gradient * gradient) + jnp.sum(ln_gradient * ln_gradient) / row_count


def shards(
    grad_blocks,
    ln_grads,
    master,
    first_moment,
    second_moment,
    average,
    ln_master,
    ln_first,
    ln_second,
    ln_average,
):
    row_count = float(lax.axis_size("row"))
    summed, ln_gradient = lax.psum(
        (grad_blocks[0].astype(jnp.float32), ln_grads[0].astype(jnp.float32)), "dp"
    )
    gradient = lax.all_to_all(summed, "col", split_axis=0, concat_axis=1, tiled=True)
    norm_total = lax.psum(squares(gradient, ln_gradient, row_count), ("row", "col"))
    clip_scale = clip_factor(norm_total)
    master_new, first_new, second_new = adam_step(
        gradient, clip_scale, first_moment, second_moment, master, decay_rate
    )
    ln_master_new, ln_first_new, ln_second_new = adam_step(
        ln_gradient, clip_scale, ln_first, ln_second, ln_master, 0.0
    )
    ln_average_new = ema_keep * ln_average + (1.0 - ema_keep) * ln_master_new
    block_master = lax.all_to_all(master_new, "col", split_axis=1, concat_axis=0, tiled=True)
    average_new = ema_keep * average + (1.0 - ema_keep) * block_master
    return (
        average_new,
        master_new,
        first_new,
        second_new,
        ln_master_new,
        ln_first_new,
        ln_second_new,
        ln_average_new,
    )


def solution(mesh):
    placed = (
        P("dp", "row", "col"),
        P("dp", None, "col"),
        P(("row", "col"), None),
        P(("row", "col"), None),
        P(("row", "col"), None),
        P("row", "col"),
        P(None, "col"),
        P(None, "col"),
        P(None, "col"),
        P(None, "col"),
    )
    return jax.shard_map(
        shards,
        mesh=mesh,
        in_specs=placed,
        out_specs=(
            P("row", "col"),
            P(("row", "col"), None),
            P(("row", "col"), None),
            P(("row", "col"), None),
            P(None, "col"),
            P(None, "col"),
            P(None, "col"),
            P(None, "col"),
        ),
        check_vma=False,
    )
```

profile of v0, /device:TPU:2, one launch (start us, length us, event | category | flops | bytes accessed | tf_op | source)
XLA Modules:
  0.0 162.7 jit_solution(14626310819225786435)
XLA Ops:
  0.6 0.7 bitcast_convert_fusion
  1.3 69.7 %all-reduce.2 = (f32[4,128,256]{2,1,0:T(8,128)}, f32[4,256]{1,0:T(4,128)S(1)}) all-reduce(bf16[4,128,256]{2,1,0:T(8,128)(2,1)} %bitcast.20, f32[4,256]{1,0:T(4,128)S(1)} %bitcast_convert_fusion), channel_id=1, replica_groups=mesh['dp'=16,'row'=8,'col'=4] {'dp'}, use_global_device_ids=true, to_apply=%region_0.0 | all-reduce | flops 132096 | bytes 794624 | tf_op jit(solution)/shard_map/psum | solution.py:53
  71.0 0.0 copy-start.1
  71.0 5.0 %all-to-all-start = ((f32[4,128,256]{2,1,0:T(8,128)}), f32[4,128,256]{2,1,0:T(8,128)S(1)}, u32[]{:S(2)}, u32[]{:S(2)}) async-start(f32[4,128,256]{2,1,0:T(8,128)} %get-tuple-element.16), calls=%async_computation | async-start | bytes 1048576 | tf_op jit(solution)/shard_map/all_to_all | solution.py:56
  76.0 0.0 copy-done.1
  76.0 0.0 copy-start.2
  76.0 0.2 copy.24
  76.2 0.8 copy-done.2
  77.0 0.2 copy.20
  77.2 0.0 copy-start.3
  77.2 0.6 multiply_reduce_fusion.1
  78.5 4.1 %all-to-all-done = f32[4,128,256]{2,1,0:T(8,128)S(1)} async-done(((f32[4,128,256]{2,1,0:T(8,128)}), f32[4,128,256]{2,1,0:T(8,128)S(1)}, u32[]{:S(2)}, u32[]{:S(2)}) %all-to-all-start) | async-done | bytes 524320 | tf_op jit(solution)/shard_map/all_to_all | solution.py:56
  82.6 0.7 multiply_reduce_fusion
  84.0 0.0 copy-done.3
  84.0 0.2 copy.22
  84.2 64.9 %psum.23 = f32[]{:T(128)} all-reduce(f32[]{:T(128)S(6)} %add.45), channel_id=1, replica_groups=mesh['dp'=16,'row'=8,'col'=4] {'row','col'}, use_global_device_ids=true, to_apply=%region_4.0 | all-reduce | flops 1 | bytes 8 | tf_op jit(solution)/shard_map/psum | solution.py:57
  149.8 0.2 copy.21
  150.0 0.4 multiply_subtract_fusion
  150.4 1.0 copy.25
  151.4 3.7 %all-to-all-start.1 = ((f32[128,4,256]{2,0,1:T(8,128)}), f32[128,4,256]{2,0,1:T(8,128)S(1)}, u32[]{:S(2)}, u32[]{:S(2)}) async-start(f32[128,4,256]{2,0,1:T(8,128)} %copy.25), calls=%async_computation.1 | async-start | bytes 1048576 | tf_op jit(solution)/shard_map/all_to_all | solution.py:66
  155.2 1.0 copy.26
  156.2 1.0 copy.27
  157.2 0.0 copy-start.4
  157.2 0.0 copy-start.5
  157.2 0.0 copy-start.6
  157.2 0.0 copy-start.7
  157.2 1.0 copy.28
  158.2 0.0 copy-done.4
  158.2 0.0 copy-done.5
  158.2 0.0 copy-done.6
  158.2 0.0 copy-done.7
  158.2 0.6 multiply_add_fusion
  158.8 0.0 copy-start
  158.8 3.0 %all-to-all-done.1 = f32[128,4,256]{2,0,1:T(8,128)S(1)} async-done(((f32[128,4,256]{2,0,1:T(8,128)}), f32[128,4,256]{2,0,1:T(8,128)S(1)}, u32[]{:S(2)}, u32[]{:S(2)}) %all-to-all-start.1) | async-done | bytes 524320 | tf_op jit(solution)/shard_map/all_to_all | solution.py:66
  161.9 0.0 copy-done
  161.9 0.9 bitcast_add_fusion
  (2 shorter events, 0.1 us)
Async XLA Ops:
  71.0 5.0 %copy-start.1 = (f32[128,1024]{1,0:T(8,128)S(1)}, f32[128,1024]{1,0:T(8,128)}, u32[]{:S(2)}) copy-start(f32[128,1024]{1,0:T(8,128)} %param.12) | copy-start | bytes 1572868
  71.0 11.6 %all-to-all-start = ((f32[4,128,256]{2,1,0:T(8,128)}), f32[4,128,256]{2,1,0:T(8,128)S(1)}, u32[]{:S(2)}, u32[]{:S(2)}) async-start(f32[4,128,256]{2,1,0:T(8,128)} %get-tuple-element.16), calls=%async_computation | async-start | bytes 1048576 | tf_op jit(solution)/shard_map/all_to_all | solution.py:56
  76.0 1.0 copy-start.2
  77.2 6.8 %copy-start.3 = (f32[128,1024]{1,0:T(8,128)S(1)}, f32[128,1024]{1,0:T(8,128)}, u32[]{:S(2)}) copy-start(f32[128,1024]{1,0:T(8,128)} %param.14) | copy-start | bytes 1572868
  151.4 10.4 %all-to-all-start.1 = ((f32[128,4,256]{2,0,1:T(8,128)}), f32[128,4,256]{2,0,1:T(8,128)S(1)}, u32[]{:S(2)}, u32[]{:S(2)}) async-start(f32[128,4,256]{2,0,1:T(8,128)} %copy.25), calls=%async_computation.1 | async-start | bytes 1048576 | tf_op jit(solution)/shard_map/all_to_all | solution.py:66
  157.2 1.0 copy-start.4
  157.2 1.0 copy-start.5
  157.2 1.0 copy-start.6
  157.2 1.0 copy-start.7
  158.8 3.0 %copy-start = (f32[512,256]{1,0:T(8,128)S(1)}, f32[512,256]{1,0:T(8,128)}, u32[]{:S(2)}) copy-start(f32[512,256]{1,0:T(8,128)} %param.15) | copy-start | bytes 1572868
where the time goes:
time: 163 us
  blocking collectives  135 us (83%)
  starting transfers between devices  8.69 us (5%)
  waiting for transfers between devices  7.11 us (4%)
  local copies, waits for them, and re-layouts  5.61 us (3%)
  other arithmetic  4.02 us (2%)
  between operations  2.72 us (2%)
    psum x1, blocking collectives, shards(): lax.psum((grad_blocks[0].astype(jnp.float32), ln_grads[0].astype(jnp.floa...  69.7 us
    psum x1, blocking collectives, shards(): lax.psum(squares(gradient, ln_gradient, row_count), ('row', 'col'))  64.9 us
    all_to_all x1, starting transfers between devices, shards(): lax.all_to_all(summed, 'col', split_axis=0, concat_axis=1, tiled=True)  4.96 us
    unnamed x22, local copies, waits for them, and re-layouts  4.42 us
    all_to_all x1, waiting for transfers between devices, shards(): lax.all_to_all(summed, 'col', split_axis=0, concat_axis=1, tiled=True)  4.12 us
    all_to_all x1, starting transfers between devices, shards(): lax.all_to_all(master_new, 'col', split_axis=1, concat_axis=0, tiled=True)  3.73 us
  transfers between devices with their start and end apart: 2, of which 2 were waited for; matrix products, arithmetic and copies ran while one was open for 3% of the time, Pallas kernels for 0%

commit v1 on v0

--- a/solution.py
+++ b/solution.py
@@ -54,7 +54,9 @@
         (grad_blocks[0].astype(jnp.float32), ln_grads[0].astype(jnp.float32)), "dp"
     )
     gradient = lax.all_to_all(summed, "col", split_axis=0, concat_axis=1, tiled=True)
-    norm_total = lax.psum(squares(gradient, ln_gradient, row_count), ("row", "col"))
+    norm_total = squares(gradient, ln_gradient, row_count)
+    for over in ("col", "row"):
+        norm_total = lax.psum(norm_total, over)
     clip_scale = clip_factor(norm_total)
     master_new, first_new, second_new = adam_step(
         gradient, clip_scale, first_moment, second_moment, master, decay_rate

time: 163 us -> 125 us (0.77)
  the two profiles are of different devices: /device:TPU:2 before, /device:TPU:1 now
where the time goes in v1:
time: 125 us
  blocking collectives  94.6 us (76%)
  waiting for transfers between devices  10.9 us (9%)
  starting transfers between devices  7.62 us (6%)
  local copies, waits for them, and re-layouts  4.77 us (4%)
  other arithmetic  4.02 us (3%)
  between operations  2.73 us (2%)
    psum x1, blocking collectives, shards(): lax.psum((grad_blocks[0].astype(jnp.float32), ln_grads[0].astype(jnp.floa...  56.8 us
    psum x2, blocking collectives, shards(): norm_total = lax.psum(norm_total, over)  37.8 us
    all_to_all x1, waiting for transfers between devices, shards(): lax.all_to_all(summed, 'col', split_axis=0, concat_axis=1, tiled=True)  5.47 us
    all_to_all x1, waiting for transfers between devices, shards(): lax.all_to_all(master_new, 'col', split_axis=1, concat_axis=0, tiled=True)  5.44 us
    all_to_all x1, starting transfers between devices, shards(): lax.all_to_all(summed, 'col', split_axis=0, concat_axis=1, tiled=True)  4.14 us
    unnamed x22, local copies, waits for them, and re-layouts  3.59 us
    all_to_all x1, starting transfers between devices, shards(): lax.all_to_all(master_new, 'col', split_axis=1, concat_axis=0, tiled=True)  3.47 us
  transfers between devices with their start and end apart: 2, of which 2 were waited for; matrix products, arithmetic and copies ran while one was open for 4% of the time, Pallas kernels for 0%

profile of v1, /device:TPU:1, one launch (start us, length us, event | category | flops | bytes accessed | tf_op | source)
XLA Modules:
  0.0 124.7 jit_solution(11046799451126062905)
XLA Ops:
  0.6 0.7 bitcast_convert_fusion
  1.3 56.8 %all-reduce.2 = (f32[4,128,256]{2,1,0:T(8,128)}, f32[4,256]{1,0:T(4,128)S(1)}) all-reduce(bf16[4,128,256]{2,1,0:T(8,128)(2,1)} %bitcast.20, f32[4,256]{1,0:T(4,128)S(1)} %bitcast_convert_fusion), channel_id=1, replica_groups=mesh['dp'=16,'row'=8,'col'=4] {'dp'}, use_global_device_ids=true, to_apply=%region_0.0 | all-reduce | flops 132096 | bytes 794624 | tf_op jit(solution)/shard_map/psum | solution.py:53
  58.1 0.0 copy-start.1
  58.1 4.1 %all-to-all-start = ((f32[4,128,256]{2,1,0:T(8,128)}), f32[4,128,256]{2,1,0:T(8,128)S(1)}, u32[]{:S(2)}, u32[]{:S(2)}) async-start(f32[4,128,256]{2,1,0:T(8,128)} %get-tuple-element.16), calls=%async_computation | async-start | bytes 1048576 | tf_op jit(solution)/shard_map/all_to_all | solution.py:56
  62.3 0.0 copy-done.1
  62.3 0.2 copy.24
  62.5 0.0 copy-start.2
  62.5 0.6 multiply_reduce_fusion.1
  63.8 5.5 %all-to-all-done = f32[4,128,256]{2,1,0:T(8,128)S(1)} async-done(((f32[4,128,256]{2,1,0:T(8,128)}), f32[4,128,256]{2,1,0:T(8,128)S(1)}, u32[]{:S(2)}, u32[]{:S(2)}) %all-to-all-start) | async-done | bytes 524320 | tf_op jit(solution)/shard_map/all_to_all | solution.py:56
  69.2 0.7 multiply_reduce_fusion
  70.6 0.0 copy-done.2
  70.6 0.0 copy-start.3
  70.6 0.2 copy.20
  70.8 7.4 %psum.30 = f32[]{:T(128)} all-reduce(f32[]{:T(128)S(6)} %add.47), channel_id=1, replica_groups=mesh['dp'=16,'row'=8,'col'=4] {'col'}, use_global_device_ids=true, to_apply=%region_4.0 | all-reduce | flops 1 | bytes 8 | tf_op jit(solution)/shard_map/psum | solution.py:59
  78.2 0.0 copy-done.3
  78.2 0.2 copy.22
  78.4 30.4 %psum.31 = f32[]{:T(128)} all-reduce(f32[]{:T(128)} %psum.30), channel_id=1, replica_groups=mesh['dp'=16,'row'=8,'col'=4] {'row'}, use_global_device_ids=true, to_apply=%region_5.0 | all-reduce | flops 1 | bytes 8 | tf_op jit(solution)/shard_map/psum | solution.py:59
  109.5 0.2 copy.21
  109.7 0.4 multiply_subtract_fusion
  110.2 1.0 copy.25
  111.2 3.5 %all-to-all-start.1 = ((f32[128,4,256]{2,0,1:T(8,128)}), f32[128,4,256]{2,0,1:T(8,128)S(1)}, u32[]{:S(2)}, u32[]{:S(2)}) async-start(f32[128,4,256]{2,0,1:T(8,128)} %copy.25), calls=%async_computation.1 | async-start | bytes 1048576 | tf_op jit(solution)/shard_map/all_to_all | solution.py:68
  114.6 1.0 copy.26
  115.6 1.0 copy.27
  116.6 0.0 copy-start.4
  116.6 0.0 copy-start.5
  116.6 0.0 copy-start.6
  116.6 0.0 copy-start.7
  116.6 1.0 copy.28
  117.6 0.0 copy-done.4
  117.6 0.0 copy-done.5
  117.6 0.0 copy-done.6
  117.6 0.0 copy-done.7
  117.7 0.6 multiply_add_fusion
  118.3 0.0 copy-start
  118.3 5.4 %all-to-all-done.1 = f32[128,4,256]{2,0,1:T(8,128)S(1)} async-done(((f32[128,4,256]{2,0,1:T(8,128)}), f32[128,4,256]{2,0,1:T(8,128)S(1)}, u32[]{:S(2)}, u32[]{:S(2)}) %all-to-all-start.1) | async-done | bytes 524320 | tf_op jit(solution)/shard_map/all_to_all | solution.py:68
  123.8 0.0 copy-done
  123.8 0.9 bitcast_add_fusion
  (2 shorter events, 0.1 us)
Async XLA Ops:
  58.1 4.1 %copy-start.1 = (f32[128,1024]{1,0:T(8,128)S(1)}, f32[128,1024]{1,0:T(8,128)}, u32[]{:S(2)}) copy-start(f32[128,1024]{1,0:T(8,128)} %param.12) | copy-start | bytes 1572868
  58.1 11.1 %all-to-all-start = ((f32[4,128,256]{2,1,0:T(8,128)}), f32[4,128,256]{2,1,0:T(8,128)S(1)}, u32[]{:S(2)}, u32[]{:S(2)}) async-start(f32[4,128,256]{2,1,0:T(8,128)} %get-tuple-element.16), calls=%async_computation | async-start | bytes 1048576 | tf_op jit(solution)/shard_map/all_to_all | solution.py:56
  62.5 8.1 %copy-start.2 = (f32[128,1024]{1,0:T(8,128)S(1)}, f32[128,1024]{1,0:T(8,128)}, u32[]{:S(2)}) copy-start(f32[128,1024]{1,0:T(8,128)} %param.13) | copy-start | bytes 1572868
  70.6 7.6 %copy-start.3 = (f32[128,1024]{1,0:T(8,128)S(1)}, f32[128,1024]{1,0:T(8,128)}, u32[]{:S(2)}) copy-start(f32[128,1024]{1,0:T(8,128)} %param.14) | copy-start | bytes 1572868
  111.2 12.6 %all-to-all-start.1 = ((f32[128,4,256]{2,0,1:T(8,128)}), f32[128,4,256]{2,0,1:T(8,128)S(1)}, u32[]{:S(2)}, u32[]{:S(2)}) async-start(f32[128,4,256]{2,0,1:T(8,128)} %copy.25), calls=%async_computation.1 | async-start | bytes 1048576 | tf_op jit(solution)/shard_map/all_to_all | solution.py:68
  116.6 1.0 copy-start.4
  116.6 1.0 copy-start.5
  116.6 1.0 copy-start.6
  116.6 1.0 copy-start.7
  118.3 5.5 %copy-start = (f32[512,256]{1,0:T(8,128)S(1)}, f32[512,256]{1,0:T(8,128)}, u32[]{:S(2)}) copy-start(f32[512,256]{1,0:T(8,128)} %param.15) | copy-start | bytes 1572868
